TPU v7x, 128 devices: a whole 4x4x4 slice. The times are simulated.
128 devices in a mesh: fronts: 8 (over y, core), rows: 16 (over z, x).
Axes of the slice: x: 4, y: 4, z: 4, core: 2. Of those that a mesh axis runs over, the one named last changes fastest.
Arguments:
- lower_rhs: float32 [16, 16384, 512], P('fronts', 'rows'), may hold values from -6 to 6
- lower_vectors: float32 [16, 16384, 256], P('fronts', 'rows')
- lower_factors: float32 [16, 16, 256, 256], P('fronts', 'rows')
- merge_vectors: float32 [16, 16, 256, 256], P('fronts', 'rows')
- merge_factors: float32 [16, 16, 256, 256], P('fronts', 'rows')
- live_blocks: int32 [16], replicated, may hold values from 1 to 16, 128 in all
- parent_front: int32 [16, 1], replicated, may hold values from 0 to 7, as said below
- front_owner: int32 [8], replicated, may hold values from 0 to 7, as said below
- contrib_rows: int32 [16, 128], replicated, may hold values from 0 to 16383, as said below
- upper_rhs: float32 [8, 16384, 512], P('fronts', 'rows'), may hold values from -6 to 6
- upper_vectors: float32 [8, 16384, 256], P('fronts', 'rows')
- upper_factors: float32 [8, 16, 256, 256], P('fronts', 'rows')
- summit_vectors: float32 [8, 16, 256, 256], P('fronts', 'rows')
- summit_factors: float32 [8, 16, 256, 256], P('fronts', 'rows')
Outputs:
- lower_result: float32 [16, 16384, 512], P('fronts', 'rows')
- upper_result: float32 [8, 16384, 512], P('fronts', 'rows')
Inputs may be any that keep to these rules, and one draw needn't show every extreme that they name: `parent_front`: every parent front has between one and 4 children, and some parent has exactly 4. `front_owner`: each parent front has its own index of fronts. `contrib_rows`: row k of a child's contribution lands in its parent's row block k // 8; no two entries are equal.
All inputs are finite; a program needn't handle non-finite values.
Results may differ from a plain program's by a relative error of at most 0.0003.
Values sent between devices are 32-bit elements; how exact they have to be, the bound alone decides.
No kernel may reach another device: no remote copies, remote signals or barrier semaphores. Data moves between devices by JAX's collectives and lax.ppermute only.
A program may use at most 128 MiB of HBM per device.

v0:
```python
import jax
import jax.numpy as jnp
from jax import lax
from jax.sharding import PartitionSpec as P

NPIV = 128
EXACT = lax.Precision.HIGHEST


def partner(value, axis, bit):
    mask = 2**bit
    pairs = [(source, source ^ mask) for source in range(lax.axis_size(axis))]
    return lax.ppermute(value, axis, pairs)


def from_root(value, axis, source):
    kept = jnp.where(lax.axis_index(axis) == source, value, 0).astype(value.dtype)
    return lax.psum(kept, axis)


def wy_apply(values, vectors, factors):
    project = jnp.einsum("fri,frn->fin", vectors, values, precision=EXACT)
    scaled = jnp.einsum("fij,fin->fjn", factors, project, precision=EXACT)
    return values - jnp.einsum("fri,fin->frn", vectors, scaled, precision=EXACT)


def combine(lead, rest, vectors, factors):
    inner = lead + jnp.einsum("fij,fin->fjn", vectors, rest, precision=EXACT)
    weight = jnp.einsum("fij,fin->fjn", factors, inner, precision=EXACT)
    return (lead - weight, rest - jnp.einsum("fij,fjn->fin", vectors, weight, precision=EXACT))


def run_tree(tops, vectors, factors, live, place):
    levels = lax.axis_size("rows").bit_length() - 1
    for level in range(levels):
        step = 1 << level
        leads = (place % (2 * step) == 0) & (place + step < live)
        follows = (place % (2 * step) == step) & (place < live)
        lead_side = leads[:, None, None]
        follow_side = follows[:, None, None]
        other, other_vectors, other_factors = partner((tops, vectors, factors), "rows", level)
        lead_part = jnp.where(lead_side, tops, other)
        rest_part = jnp.where(lead_side, other, tops)
        node_vectors = jnp.where(lead_side, other_vectors, vectors)
        node_factors = jnp.where(lead_side, other_factors, factors)
        lead_new, rest_new = combine(lead_part, rest_part, node_vectors, node_factors)
        tops = jnp.where(lead_side, lead_new, jnp.where(follow_side, rest_new, tops))
    return tops


def per_device(
    lower_rhs,
    lower_vectors,
    lower_factors,
    merge_vectors,
    merge_factors,
    live_blocks,
    parent_front,
    front_owner,
    contrib_rows,
    upper_rhs,
    upper_vectors,
    upper_factors,
    summit_vectors,
    summit_factors,
):
    place = lax.axis_index("rows")
    column = lax.axis_index("fronts")
    blocks = lax.axis_size("rows")
    local_fronts = lower_rhs.shape[0]
    height = lower_rhs.shape[1]
    width = lower_factors.shape[-1]
    live = lax.dynamic_slice_in_dim(live_blocks, column * local_fronts, local_fronts)
    applied = wy_apply(lower_rhs, lower_vectors, lower_factors[:, 0])
    applied = jnp.where((place < live)[:, None, None], applied, lower_rhs)
    tops = run_tree(applied[:, :width], merge_vectors[:, 0], merge_factors[:, 0], live, place)
    keep = (jnp.arange(width) < NPIV)[None, :, None] | (place != 0)
    lower_result = jnp.concatenate([jnp.where(keep, tops, 0.0), applied[:, width:]], axis=1)
    contrib = tops[:, NPIV:]
    share = (width - NPIV) // blocks
    shared = from_root(contrib, "rows", 0)
    gathered = lax.all_gather(shared, "fronts", axis=0, tiled=True)
    front_portions = lax.dynamic_slice_in_dim(gathered, place * share, share, 1)
    parents = jnp.arange(front_owner.shape[0], dtype=jnp.int32)
    target = jnp.sum(jnp.where(parent_front == parents[None, :], front_owner[None, :], 0), axis=1)
    rows_here = lax.dynamic_slice_in_dim(contrib_rows, place * share, share, 1) - place * height
    rows_here = jnp.where((target == column)[:, None], rows_here, -1).reshape(-1)
    selector = (
        lax.broadcasted_iota(jnp.int32, (height, rows_here.shape[0]), 0) == rows_here[None, :]
    ).astype(jnp.float32)
    positioned_rows = jnp.dot(
        selector,
        front_portions.reshape(-1, front_portions.shape[-1]),
        precision=EXACT,
        preferred_element_type=jnp.float32,
    )
    taken = jnp.max(selector, axis=1) > 0
    assembled = jnp.where(taken[:, None], positioned_rows, upper_rhs[0])[None]
    upper_applied = wy_apply(assembled, upper_vectors, upper_factors[:, 0])
    whole = jnp.full((1,), blocks, jnp.int32)
    upper_tops = run_tree(
        upper_applied[:, :width], summit_vectors[:, 0], summit_factors[:, 0], whole, place
    )
    upper_result = jnp.concatenate([upper_tops, upper_applied[:, width:]], axis=1)
    return (lower_result, upper_result)


def solution(mesh):
    placed = (
        P("fronts", "rows", None),
        P("fronts", "rows", None),
        P("fronts", "rows", None, None),
        P("fronts", "rows", None, None),
        P("fronts", "rows", None, None),
        P(),
        P(),
        P(),
        P(),
        P("fronts", "rows", None),
        P("fronts", "rows", None),
        P("fronts", "rows", None, None),
        P("fronts", "rows", None, None),
        P("fronts", "rows", None, None),
    )
    return jax.shard_map(
        per_device,
        mesh=mesh,
        in_specs=placed,
        out_specs=(P("fronts", "rows", None), P("fronts", "rows", None)),
        check_vma=False,
    )
```

profile of v0, /device:TPU:0, one launch (start us, length us, event | category | flops | bytes accessed | tf_op | source)
XLA Modules:
  0.0 505.6 jit_solution(8171327496330712370)
XLA Ops:
  7.2 5.5 %copy.94 = f32[2,1024,512]{1,2,0:T(8,128)} copy(f32[2,1024,512]{2,1,0:T(8,128)} %param.14) | data formatting | bytes 8388608 | tf_op args[0]
  12.7 8.5 %fusion.110 = f32[2,256,512]{1,2,0:T(8,128)S(1)} fusion(f32[2,1024,256]{2,1,0:T(8,128)S(1)} %copy-done, f32[2,1024,512]{2,1,0:T(8,128)} %param.14), kind=kOutput, calls=%fused_computation.174 | convolution fusion | flops 3221225472 | bytes 7340032 | tf_op jit(solution)/shard_map/fri,frn->fin/dot_general | solution.py:22
  23.5 5.6 %subtract_select_fusion = f32[2,1024,512]{1,2,0:T(8,128)S(1)} fusion(f32[2,1024,512]{1,2,0:T(8,128)} %copy.94, f32[2,512,256]{2,1,0:T(8,128)S(1)} %fusion.32, f32[2,1024,256]{2,1,0:T(8,128)S(1)} %copy-done, pred[2]{0:T(512)(128)(4,1)S(1)} %get-tuple-element.11), kind=kOutput, calls=%fused_computation | convolution fusion | flops 3223322624 | bytes 11534338 | tf_op jit(solution)/shard_map/fri,fin->frn/dot_general | solution.py:24
  34.0 33.7 %collective-permute-done.2 = f32[2,256,256]{2,1,0:T(8,128)S(1)} collective-permute-done((f32[2,256,256]{2,1,0:T(8,128)S(1)}, f32[2,256,256]{2,1,0:T(8,128)S(1)}, u32[]{:S(2)}, u32[]{:S(2)}) %collective-permute-start.2) | collective-permute-done | bytes 524320 | tf_op jit(solution)/shard_map/ppermute | solution.py:13
  68.5 3.3 convolution_add_fusion.3
  71.8 5.9 %collective-permute-done.1 = f32[2,256,256]{2,1,0:T(8,128)} collective-permute-done((f32[2,256,256]{2,1,0:T(8,128)S(1)}, f32[2,256,256]{2,1,0:T(8,128)}, u32[]{:S(2)}, u32[]{:S(2)}) %collective-permute-start.1) | collective-permute-done | bytes 524320 | tf_op jit(solution)/shard_map/ppermute | solution.py:13
  82.0 4.1 subtract_select_fusion.4
  86.1 3.4 collective-permute-start.3
  89.8 3.3 collective-permute-start.4
  93.0 32.0 %collective-permute-done.5 = f32[2,256,256]{2,1,0:T(8,128)S(1)} collective-permute-done((f32[2,256,256]{2,1,0:T(8,128)S(1)}, f32[2,256,256]{2,1,0:T(8,128)S(1)}, u32[]{:S(2)}, u32[]{:S(2)}) %collective-permute-start.5) | collective-permute-done | bytes 524320 | tf_op jit(solution)/shard_map/ppermute | solution.py:13
  126.4 7.9 %collective-permute-done.4 = f32[2,256,256]{2,1,0:T(8,128)S(1)} collective-permute-done((f32[2,256,256]{2,1,0:T(8,128)S(1)}, f32[2,256,256]{2,1,0:T(8,128)S(1)}, u32[]{:S(2)}, u32[]{:S(2)}) %collective-permute-start.4) | collective-permute-done | bytes 524320 | tf_op jit(solution)/shard_map/ppermute | solution.py:13
  137.6 4.1 subtract_select_fusion.3
  146.1 33.0 %collective-permute-done.8 = f32[2,256,256]{2,1,0:T(8,128)S(1)} collective-permute-done((f32[2,256,256]{2,1,0:T(8,128)S(1)}, f32[2,256,256]{2,1,0:T(8,128)S(1)}, u32[]{:S(2)}, u32[]{:S(2)}) %collective-permute-start.8) | collective-permute-done | bytes 524320 | tf_op jit(solution)/shard_map/ppermute | solution.py:13
  180.5 7.3 %collective-permute-done.7 = f32[2,256,256]{2,1,0:T(8,128)S(1)} collective-permute-done((f32[2,256,256]{2,1,0:T(8,128)S(1)}, f32[2,256,256]{2,1,0:T(8,128)S(1)}, u32[]{:S(2)}, u32[]{:S(2)}) %collective-permute-start.7) | collective-permute-done | bytes 524320 | tf_op jit(solution)/shard_map/ppermute | solution.py:13
  191.1 4.1 subtract_select_fusion.2
  195.2 3.8 collective-permute-start.9
  199.1 3.4 collective-permute-start.10
  202.5 31.8 %collective-permute-done.11 = f32[2,256,256]{2,1,0:T(8,128)} collective-permute-done((f32[2,256,256]{2,1,0:T(8,128)S(1)}, f32[2,256,256]{2,1,0:T(8,128)}, u32[]{:S(2)}, u32[]{:S(2)}) %collective-permute-start.11) | collective-permute-done | bytes 524320 | tf_op jit(solution)/shard_map/ppermute | solution.py:13
  237.0 5.1 %collective-permute-done.10 = f32[2,256,256]{2,1,0:T(8,128)} collective-permute-done((f32[2,256,256]{2,1,0:T(8,128)S(1)}, f32[2,256,256]{2,1,0:T(8,128)}, u32[]{:S(2)}, u32[]{:S(2)}) %collective-permute-start.10) | collective-permute-done | bytes 524320 | tf_op jit(solution)/shard_map/ppermute | solution.py:13
  246.5 5.0 broadcast_select_fusion
  252.8 87.2 %all-reduce.2.cloned.1.call-done = f32[2,128,512]{1,2,0:T(8,128)} async-done(((f32[2,128,512]{1,2,0:T(8,128)}), f32[2,128,512]{1,2,0:T(8,128)}) %all-reduce.2.cloned.1.call-update) | async-done | bytes 524304 | tf_op jit(solution)/shard_map/psum | solution.py:18
  342.5 31.2 %all-gather.2.cloned.1.call-done = f32[16,128,512]{2,1,0:T(8,128)} async-done(((f32[2,128,512]{2,1,0:T(8,128)}), f32[16,128,512]{2,1,0:T(8,128)}) %all-gather.2.cloned.1.call-update) | async-done | bytes 4194320 | tf_op jit(solution)/shard_map/all_gather | solution.py:82
  376.5 3.4 fusion.22
  386.8 17.1 %collective-permute-done.14 = f32[1,256,256]{2,1,0:T(8,128)S(1)} collective-permute-done((f32[1,256,256]{2,1,0:T(8,128)S(1)}, f32[1,256,256]{2,1,0:T(8,128)S(1)}, u32[]{:S(2)}, u32[]{:S(2)}) %collective-permute-start.14) | collective-permute-done | bytes 262176 | tf_op jit(solution)/shard_map/ppermute | solution.py:13
  415.8 3.1 collective-permute-start.16
  418.9 15.4 %collective-permute-done.17 = f32[1,256,256]{2,1,0:T(8,128)} collective-permute-done((f32[1,256,256]{2,1,0:T(8,128)S(1)}, f32[1,256,256]{2,1,0:T(8,128)}, u32[]{:S(2)}, u32[]{:S(2)}) %collective-permute-start.17) | collective-permute-done | bytes 262176 | tf_op jit(solution)/shard_map/ppermute | solution.py:13
  445.5 16.8 %collective-permute-done.20 = f32[1,256,256]{2,1,0:T(8,128)S(1)} collective-permute-done((f32[1,256,256]{2,1,0:T(8,128)S(1)}, f32[1,256,256]{2,1,0:T(8,128)S(1)}, u32[]{:S(2)}, u32[]{:S(2)}) %collective-permute-start.20) | collective-permute-done | bytes 262176 | tf_op jit(solution)/shard_map/ppermute | solution.py:13
  469.1 3.2 collective-permute-start.21
  472.7 3.2 collective-permute-start.22
  475.9 3.7 slice.21
  479.6 4.8 pad_maximum_fusion
  484.4 5.4 %copy.126 = f32[2,1024,512]{2,1,0:T(8,128)} copy(f32[2,1024,512]{1,2,0:T(8,128)} %pad_maximum_fusion) | data formatting | bytes 8388608
  (132 shorter events, 85.5 us)
Async XLA Ops:
  7.2 5.6 %copy-start = (f32[2,1024,256]{2,1,0:T(8,128)S(1)}, f32[2,1024,256]{2,1,0:T(8,128)}, u32[]{:S(2)}) copy-start(f32[2,1024,256]{2,1,0:T(8,128)} %param.15) | copy-start | bytes 6291460
  7.2 332.8 %all-reduce.2.cloned.1.call-start = ((), (), s32[]{:S(2)}) async-start(), calls=%async_computation | async-start | bytes 1048576 | tf_op jit(solution)/shard_map/psum | solution.py:18
  30.2 37.5 %collective-permute-start = (f32[2,256,512]{1,2,0:T(8,128)}, f32[2,256,512]{1,2,0:T(8,128)S(1)}, u32[]{:S(2)}, u32[]{:S(2)}) collective-permute-start(f32[2,256,512]{1,2,0:T(8,128)} %slice.20), channel_id=1, source_target_pairs={{0,1},{1,0},{2,3},{3,2},{4,5},{5,4},{6,7},{7,6},{8,9},{9,8},{10,11... | collective-permute-start | bytes 3145736 | tf_op jit(solution)/shard_map/ppermute | solution.py:13
  31.8 35.9 %collective-permute-start.2 = (f32[2,256,256]{2,1,0:T(8,128)S(1)}, f32[2,256,256]{2,1,0:T(8,128)S(1)}, u32[]{:S(2)}, u32[]{:S(2)}) collective-permute-start(f32[2,256,256]{2,1,0:T(8,128)S(1)} %bitcast.283), channel_id=1, source_target_pairs={{0,1},{1,0},{2,3},{3,2},{4,5},{5,4},{6,7},{7,6},{8,9},{9,8},{10,11... | collective-permute-start | bytes 1572872 | tf_op jit(solution)/shard_map/ppermute | solution.py:13
  33.0 44.7 %collective-permute-start.1 = (f32[2,256,256]{2,1,0:T(8,128)S(1)}, f32[2,256,256]{2,1,0:T(8,128)}, u32[]{:S(2)}, u32[]{:S(2)}) collective-permute-start(f32[2,256,256]{2,1,0:T(8,128)S(1)} %bitcast.291), channel_id=1, source_target_pairs={{0,1},{1,0},{2,3},{3,2},{4,5},{5,4},{6,7},{7,6},{8,9},{9,8},{10,11... | collective-permute-start | bytes 1572872 | tf_op jit(solution)/shard_map/ppermute | solution.py:13
  86.1 38.9 %collective-permute-start.3 = (f32[2,256,512]{1,2,0:T(8,128)S(1)}, f32[2,256,512]{1,2,0:T(8,128)S(1)}, u32[]{:S(2)}, u32[]{:S(2)}) collective-permute-start(f32[2,256,512]{1,2,0:T(8,128)S(1)} %subtract_select_fusion.4), channel_id=1, source_target_pairs={{0,2},{1,3},{2,0},{3,1},{4,6},{5,7},{6,4},{7,5},{8,10},{9,11},{10,... | collective-permute-start | bytes 3145736 | tf_op jit(solution)/shard_map/ppermute | solution.py:13
  89.5 35.5 %collective-permute-start.5 = (f32[2,256,256]{2,1,0:T(8,128)S(1)}, f32[2,256,256]{2,1,0:T(8,128)S(1)}, u32[]{:S(2)}, u32[]{:S(2)}) collective-permute-start(f32[2,256,256]{2,1,0:T(8,128)S(1)} %bitcast.284), channel_id=1, source_target_pairs={{0,2},{1,3},{2,0},{3,1},{4,6},{5,7},{6,4},{7,5},{8,10},{9,11},{10,... | collective-permute-start | bytes 1572872 | tf_op jit(solution)/shard_map/ppermute | solution.py:13
  89.8 44.5 %collective-permute-start.4 = (f32[2,256,256]{2,1,0:T(8,128)S(1)}, f32[2,256,256]{2,1,0:T(8,128)S(1)}, u32[]{:S(2)}, u32[]{:S(2)}) collective-permute-start(f32[2,256,256]{2,1,0:T(8,128)S(1)} %bitcast.292), channel_id=1, source_target_pairs={{0,2},{1,3},{2,0},{3,1},{4,6},{5,7},{6,4},{7,5},{8,10},{9,11},{10,... | collective-permute-start | bytes 1572872 | tf_op jit(solution)/shard_map/ppermute | solution.py:13
  141.7 37.5 %collective-permute-start.6 = (f32[2,256,512]{1,2,0:T(8,128)S(1)}, f32[2,256,512]{1,2,0:T(8,128)S(1)}, u32[]{:S(2)}, u32[]{:S(2)}) collective-permute-start(f32[2,256,512]{1,2,0:T(8,128)S(1)} %subtract_select_fusion.3), channel_id=1, source_target_pairs={{0,4},{1,5},{2,6},{3,7},{4,0},{5,1},{6,2},{7,3},{8,12},{9,13},{10,... | collective-permute-start | bytes 3145736 | tf_op jit(solution)/shard_map/ppermute | solution.py:13
  143.9 35.2 %collective-permute-start.8 = (f32[2,256,256]{2,1,0:T(8,128)S(1)}, f32[2,256,256]{2,1,0:T(8,128)S(1)}, u32[]{:S(2)}, u32[]{:S(2)}) collective-permute-start(f32[2,256,256]{2,1,0:T(8,128)S(1)} %bitcast.285), channel_id=1, source_target_pairs={{0,4},{1,5},{2,6},{3,7},{4,0},{5,1},{6,2},{7,3},{8,12},{9,13},{10,... | collective-permute-start | bytes 1572872 | tf_op jit(solution)/shard_map/ppermute | solution.py:13
  144.2 43.6 %collective-permute-start.7 = (f32[2,256,256]{2,1,0:T(8,128)S(1)}, f32[2,256,256]{2,1,0:T(8,128)S(1)}, u32[]{:S(2)}, u32[]{:S(2)}) collective-permute-start(f32[2,256,256]{2,1,0:T(8,128)S(1)} %bitcast.293), channel_id=1, source_target_pairs={{0,4},{1,5},{2,6},{3,7},{4,0},{5,1},{6,2},{7,3},{8,12},{9,13},{10,... | collective-permute-start | bytes 1572872 | tf_op jit(solution)/shard_map/ppermute | solution.py:13
  195.2 39.1 %collective-permute-start.9 = (f32[2,256,512]{1,2,0:T(8,128)S(1)}, f32[2,256,512]{1,2,0:T(8,128)S(1)}, u32[]{:S(2)}, u32[]{:S(2)}) collective-permute-start(f32[2,256,512]{1,2,0:T(8,128)S(1)} %subtract_select_fusion.2), channel_id=1, source_target_pairs={{0,8},{1,9},{2,10},{3,11},{4,12},{5,13},{6,14},{7,15},{8,0},{9,1},... | collective-permute-start | bytes 3145736 | tf_op jit(solution)/shard_map/ppermute | solution.py:13
  199.0 35.4 %collective-permute-start.11 = (f32[2,256,256]{2,1,0:T(8,128)S(1)}, f32[2,256,256]{2,1,0:T(8,128)}, u32[]{:S(2)}, u32[]{:S(2)}) collective-permute-start(f32[2,256,256]{2,1,0:T(8,128)S(1)} %bitcast.286), channel_id=1, source_target_pairs={{0,8},{1,9},{2,10},{3,11},{4,12},{5,13},{6,14},{7,15},{8,0},{9,1},... | collective-permute-start | bytes 1572872 | tf_op jit(solution)/shard_map/ppermute | solution.py:13
  199.1 43.1 %collective-permute-start.10 = (f32[2,256,256]{2,1,0:T(8,128)S(1)}, f32[2,256,256]{2,1,0:T(8,128)}, u32[]{:S(2)}, u32[]{:S(2)}) collective-permute-start(f32[2,256,256]{2,1,0:T(8,128)S(1)} %bitcast.294), channel_id=1, source_target_pairs={{0,8},{1,9},{2,10},{3,11},{4,12},{5,13},{6,14},{7,15},{8,0},{9,1},... | collective-permute-start | bytes 1572872 | tf_op jit(solution)/shard_map/ppermute | solution.py:13
  251.5 90.6 %copy-start.25 = (s32[8]{0:T(128)S(1)}, s32[8]{0:T(128)}, u32[]{:S(2)}) copy-start(s32[8]{0:T(128)} %param.21) | copy-start | bytes 100
  251.5 90.6 %copy-start.26 = (s32[16,1]{0,1:T(1,128)S(1)}, s32[16,1]{0,1:T(1,128)}, u32[]{:S(2)}) copy-start(s32[16,1]{0,1:T(1,128)} %param.20) | copy-start | bytes 196
  251.5 90.7 %copy-start.23 = (s32[16,128]{1,0:T(8,128)S(1)}, s32[16,128]{1,0:T(8,128)}, u32[]{:S(2)}) copy-start(s32[16,128]{1,0:T(8,128)} %param.22) | copy-start | bytes 24580
  252.3 121.4 %all-gather.2.cloned.1.call-start = ((), (), s32[]{:S(2)}) async-start(), calls=%async_computation.1 | async-start | bytes 4718592 | tf_op jit(solution)/shard_map/all_gather | solution.py:82
  342.5 33.9 %copy-start.10 = (f32[1,1024,256]{2,1,0:T(8,128)S(1)}, f32[1,1024,256]{2,1,0:T(8,128)}, u32[]{:S(2)}) copy-start(f32[1,1024,256]{2,1,0:T(8,128)} %param.24) | copy-start | bytes 3145732
  383.3 20.6 %collective-permute-start.12 = (f32[1,256,512]{2,1,0:T(8,128)}, f32[1,256,512]{2,1,0:T(8,128)S(1)}, u32[]{:S(2)}, u32[]{:S(2)}) collective-permute-start(f32[1,256,512]{2,1,0:T(8,128)} %slice.23), channel_id=1, source_target_pairs={{0,1},{1,0},{2,3},{3,2},{4,5},{5,4},{6,7},{7,6},{8,9},{9,8},{10,11... | collective-permute-start | bytes 1572872 | tf_op jit(solution)/shard_map/ppermute | solution.py:13
  384.8 25.6 %copy-start.6 = (f32[1,1024,512]{2,1,0:T(8,128)S(1)}, f32[1,1024,512]{2,1,0:T(8,128)}, u32[]{:S(2)}) copy-start(f32[1,1024,512]{2,1,0:T(8,128)} %copy-done.5) | copy-start | bytes 6291460
  384.8 19.1 %collective-permute-start.14 = (f32[1,256,256]{2,1,0:T(8,128)S(1)}, f32[1,256,256]{2,1,0:T(8,128)S(1)}, u32[]{:S(2)}, u32[]{:S(2)}) collective-permute-start(f32[1,256,256]{2,1,0:T(8,128)S(1)} %bitcast.287), channel_id=1, source_target_pairs={{0,1},{1,0},{2,3},{3,2},{4,5},{5,4},{6,7},{7,6},{8,9},{9,8},{10,11... | collective-permute-start | bytes 786440 | tf_op jit(solution)/shard_map/ppermute | solution.py:13
  385.4 23.4 %collective-permute-start.13 = (f32[1,256,256]{2,1,0:T(8,128)}, f32[1,256,256]{2,1,0:T(8,128)S(1)}, u32[]{:S(2)}, u32[]{:S(2)}) collective-permute-start(f32[1,256,256]{2,1,0:T(8,128)} %bitcast.11), channel_id=1, source_target_pairs={{0,1},{1,0},{2,3},{3,2},{4,5},{5,4},{6,7},{7,6},{8,9},{9,8},{10,11... | collective-permute-start | bytes 786440 | tf_op jit(solution)/shard_map/ppermute | solution.py:13
  412.1 22.1 %collective-permute-start.15 = (f32[1,256,512]{2,1,0:T(8,128)S(1)}, f32[1,256,512]{2,1,0:T(8,128)S(1)}, u32[]{:S(2)}, u32[]{:S(2)}) collective-permute-start(f32[1,256,512]{2,1,0:T(8,128)S(1)} %fusion.30), channel_id=1, source_target_pairs={{0,2},{1,3},{2,0},{3,1},{4,6},{5,7},{6,4},{7,5},{8,10},{9,11},{10,... | collective-permute-start | bytes 1572872 | tf_op jit(solution)/shard_map/ppermute | solution.py:13
  415.2 19.0 %collective-permute-start.17 = (f32[1,256,256]{2,1,0:T(8,128)S(1)}, f32[1,256,256]{2,1,0:T(8,128)}, u32[]{:S(2)}, u32[]{:S(2)}) collective-permute-start(f32[1,256,256]{2,1,0:T(8,128)S(1)} %bitcast.288), channel_id=1, source_target_pairs={{0,2},{1,3},{2,0},{3,1},{4,6},{5,7},{6,4},{7,5},{8,10},{9,11},{10,... | collective-permute-start | bytes 786440 | tf_op jit(solution)/shard_map/ppermute | solution.py:13
  415.8 22.5 %collective-permute-start.16 = (f32[1,256,256]{2,1,0:T(8,128)}, f32[1,256,256]{2,1,0:T(8,128)}, u32[]{:S(2)}, u32[]{:S(2)}) collective-permute-start(f32[1,256,256]{2,1,0:T(8,128)} %bitcast.11), channel_id=1, source_target_pairs={{0,2},{1,3},{2,0},{3,1},{4,6},{5,7},{6,4},{7,5},{8,10},{9,11},{10,... | collective-permute-start | bytes 786440 | tf_op jit(solution)/shard_map/ppermute | solution.py:13
  441.8 21.2 %collective-permute-start.18 = (f32[1,256,512]{2,1,0:T(8,128)S(1)}, f32[1,256,512]{2,1,0:T(8,128)}, u32[]{:S(2)}, u32[]{:S(2)}) collective-permute-start(f32[1,256,512]{2,1,0:T(8,128)S(1)} %fusion.28), channel_id=1, source_target_pairs={{0,4},{1,5},{2,6},{3,7},{4,0},{5,1},{6,2},{7,3},{8,12},{9,13},{10,... | collective-permute-start | bytes 1572872 | tf_op jit(solution)/shard_map/ppermute | solution.py:13
  443.5 18.9 %collective-permute-start.20 = (f32[1,256,256]{2,1,0:T(8,128)S(1)}, f32[1,256,256]{2,1,0:T(8,128)S(1)}, u32[]{:S(2)}, u32[]{:S(2)}) collective-permute-start(f32[1,256,256]{2,1,0:T(8,128)S(1)} %bitcast.289), channel_id=1, source_target_pairs={{0,4},{1,5},{2,6},{3,7},{4,0},{5,1},{6,2},{7,3},{8,12},{9,13},{10,... | collective-permute-start | bytes 786440 | tf_op jit(solution)/shard_map/ppermute | solution.py:13
  444.0 21.7 %collective-permute-start.19 = (f32[1,256,256]{2,1,0:T(8,128)}, f32[1,256,256]{2,1,0:T(8,128)}, u32[]{:S(2)}, u32[]{:S(2)}) collective-permute-start(f32[1,256,256]{2,1,0:T(8,128)} %bitcast.11), channel_id=1, source_target_pairs={{0,4},{1,5},{2,6},{3,7},{4,0},{5,1},{6,2},{7,3},{8,12},{9,13},{10,... | collective-permute-start | bytes 786440 | tf_op jit(solution)/shard_map/ppermute | solution.py:13
  469.1 21.6 %collective-permute-start.21 = (f32[1,256,512]{2,1,0:T(8,128)S(1)}, f32[1,256,512]{2,1,0:T(8,128)S(1)}, u32[]{:S(2)}, u32[]{:S(2)}) collective-permute-start(f32[1,256,512]{2,1,0:T(8,128)S(1)} %fusion.26), channel_id=1, source_target_pairs={{0,8},{1,9},{2,10},{3,11},{4,12},{5,13},{6,14},{7,15},{8,0},{9,1},... | collective-permute-start | bytes 1572872 | tf_op jit(solution)/shard_map/ppermute | solution.py:13
  472.3 18.4 %collective-permute-start.23 = (f32[1,256,256]{2,1,0:T(8,128)S(1)}, f32[1,256,256]{2,1,0:T(8,128)}, u32[]{:S(2)}, u32[]{:S(2)}) collective-permute-start(f32[1,256,256]{2,1,0:T(8,128)S(1)} %bitcast.290), channel_id=1, source_target_pairs={{0,8},{1,9},{2,10},{3,11},{4,12},{5,13},{6,14},{7,15},{8,0},{9,1},... | collective-permute-start | bytes 786440 | tf_op jit(solution)/shard_map/ppermute | solution.py:13
  472.7 20.8 %collective-permute-start.22 = (f32[1,256,256]{2,1,0:T(8,128)}, f32[1,256,256]{2,1,0:T(8,128)}, u32[]{:S(2)}, u32[]{:S(2)}) collective-permute-start(f32[1,256,256]{2,1,0:T(8,128)} %bitcast.11), channel_id=1, source_target_pairs={{0,8},{1,9},{2,10},{3,11},{4,12},{5,13},{6,14},{7,15},{8,0},{9,1},... | collective-permute-start | bytes 786440 | tf_op jit(solution)/shard_map/ppermute | solution.py:13
  (22 other events, 58.5 us)
Sparse Core Ops, SparseCore 0:
  252.5 87.4 all-reduce.1
  342.3 31.4 all-gather.1
where the time goes:
time: 512 us; the launch traced here: 506 us
  waiting for transfers between devices  332 us (65%)
  matrix products  81.7 us (16%)
  starting transfers between devices  43.5 us (8%)
  local copies, waits for them, and re-layouts  25.6 us (5%)
  between operations  14.8 us (3%)
  other arithmetic  7.53 us (1%)
    ppermute x24, waiting for transfers between devices, partner(): return lax.ppermute(value, axis, pairs)  214 us
    psum x1, waiting for transfers between devices, from_root(): return lax.psum(kept, axis)  87.2 us
    ppermute x24, starting transfers between devices, partner(): return lax.ppermute(value, axis, pairs)  43 us
    all_gather x1, waiting for transfers between devices, per_device(): gathered = lax.all_gather(shared, 'fronts', axis=0, tiled=True)  31.2 us
    dot_general x8, matrix products, combine(): jnp.einsum('fij,fjn->fin', vectors, weight, precision=EXACT)  24.5 us
    dot_general x8, matrix products, combine(): weight = jnp.einsum('fij,fin->fjn', factors, inner, precision=EXACT)  16.4 us
    dot_general x8, matrix products, combine(): inner = lead + jnp.einsum('fij,fin->fjn', vectors, rest, precision=EXACT)  16 us
    unnamed x56, local copies, waits for them, and re-layouts  12.5 us
  transfers between devices with their start and end apart: 26, of which 18 were waited for; matrix products, arithmetic and copies ran while one was open for 6% of the time, Pallas kernels for 0%

commit v1 on v0

--- a/solution.py
+++ b/solution.py
@@ -79,7 +79,10 @@
     contrib = tops[:, NPIV:]
     share = (width - NPIV) // blocks
     shared = from_root(contrib, "rows", 0)
-    gathered = lax.all_gather(shared, "fronts", axis=0, tiled=True)
+    devices = lax.axis_size("fronts")
+    pieces = jnp.stack([shared for _ in range(devices)])
+    pieces = lax.all_to_all(pieces, "fronts", split_axis=0, concat_axis=0)
+    gathered = jnp.concatenate(pieces, axis=0)
     front_portions = lax.dynamic_slice_in_dim(gathered, place * share, share, 1)
     parents = jnp.arange(front_owner.shape[0], dtype=jnp.int32)
     target = jnp.sum(jnp.where(parent_front == parents[None, :], front_owner[None, :], 0), axis=1)

time: 512 us -> 533 us (1.041)
  waiting for transfers between devices: 332 us -> 352 us
    all_to_all x0 -> x1, waiting for transfers between devices: none -> 49.2 us  [per_device(): pieces = lax.all_to_all(pieces, 'fronts', split_axis=0, concat_axis=0)]
    all_gather x1 -> x0, waiting for transfers between devices: 31.2 us -> none  [per_device(): gathered = lax.all_gather(shared, 'fronts', axis=0, tiled=True)]
    unnamed x56 -> x60, local copies, waits for them, and re-layouts: 12.5 us -> 12.5 us
  transfers between devices with their start and end apart: 26 -> 26, of which waited for: 18 -> 18; matrix products, arithmetic and copies ran while one was open for 6% -> 5% of each run, Pallas kernels for 0% -> 0%
where the time goes in v1:
time: 533 us; the launch traced here: 527 us
  waiting for transfers between devices  352 us (66%)
  matrix products  80.9 us (15%)
  starting transfers between devices  45.9 us (9%)
  local copies, waits for them, and re-layouts  25.5 us (5%)
  between operations  14.8 us (3%)
  other arithmetic  7.52 us (1%)
    ppermute x24, waiting for transfers between devices, partner(): return lax.ppermute(value, axis, pairs)  215 us
    psum x1, waiting for transfers between devices, from_root(): return lax.psum(kept, axis)  87.7 us
    all_to_all x1, waiting for transfers between devices, per_device(): pieces = lax.all_to_all(pieces, 'fronts', split_axis=0, concat_axis=0)  49.2 us
    ppermute x24, starting transfers between devices, partner(): return lax.ppermute(value, axis, pairs)  40.7 us
    dot_general x8, matrix products, combine(): jnp.einsum('fij,fjn->fin', vectors, weight, precision=EXACT)  24.4 us
    dot_general x8, matrix products, combine(): weight = jnp.einsum('fij,fin->fjn', factors, inner, precision=EXACT)  16.6 us
    dot_general x8, matrix products, combine(): inner = lead + jnp.einsum('fij,fin->fjn', vectors, rest, precision=EXACT)  16 us
    unnamed x60, local copies, waits for them, and re-layouts  12.5 us
  transfers between devices with their start and end apart: 26, of which 18 were waited for; matrix products, arithmetic and copies ran while one was open for 5% of the time, Pallas kernels for 0%

profile of v1, /device:TPU:0, one launch (start us, length us, event | category | flops | bytes accessed | tf_op | source)
XLA Modules:
  0.0 526.6 jit_solution(2491099389419857637)
XLA Ops:
  7.2 5.5 %copy.60 = f32[2,1024,512]{1,2,0:T(8,128)} copy(f32[2,1024,512]{2,1,0:T(8,128)} %param.14) | data formatting | bytes 8388608 | tf_op args[0]
  12.7 8.6 %fusion.110 = f32[2,256,512]{1,2,0:T(8,128)S(1)} fusion(f32[2,1024,256]{2,1,0:T(8,128)S(1)} %copy-done, f32[2,1024,512]{2,1,0:T(8,128)} %param.14), kind=kOutput, calls=%fused_computation.174 | convolution fusion | flops 3221225472 | bytes 7340032 | tf_op jit(solution)/shard_map/fri,frn->fin/dot_general | solution.py:22
  22.5 5.6 %subtract_select_fusion = f32[2,1024,512]{1,2,0:T(8,128)S(1)} fusion(f32[2,1024,512]{1,2,0:T(8,128)} %copy.60, f32[2,512,256]{2,1,0:T(8,128)S(1)} %fusion.32, f32[2,1024,256]{2,1,0:T(8,128)S(1)} %copy-done, pred[2]{0:T(512)(128)(4,1)S(1)} %get-tuple-element.9), kind=kOutput, calls=%fused_computation | convolution fusion | flops 3223322624 | bytes 11534338 | tf_op jit(solution)/shard_map/fri,fin->frn/dot_general | solution.py:24
  33.1 33.7 %collective-permute-done.2 = f32[2,256,256]{2,1,0:T(8,128)S(1)} collective-permute-done((f32[2,256,256]{2,1,0:T(8,128)S(1)}, f32[2,256,256]{2,1,0:T(8,128)S(1)}, u32[]{:S(2)}, u32[]{:S(2)}) %collective-permute-start.2) | collective-permute-done | bytes 524320 | tf_op jit(solution)/shard_map/ppermute | solution.py:13
  67.5 3.3 convolution_add_fusion.3
  70.9 5.9 %collective-permute-done.1 = f32[2,256,256]{2,1,0:T(8,128)} collective-permute-done((f32[2,256,256]{2,1,0:T(8,128)S(1)}, f32[2,256,256]{2,1,0:T(8,128)}, u32[]{:S(2)}, u32[]{:S(2)}) %collective-permute-start.1) | collective-permute-done | bytes 524320 | tf_op jit(solution)/shard_map/ppermute | solution.py:13
  76.8 3.0 fusion.40
  81.1 4.1 subtract_select_fusion.4
  85.2 3.4 collective-permute-start.3
  88.8 3.3 collective-permute-start.4
  92.1 32.0 %collective-permute-done.5 = f32[2,256,256]{2,1,0:T(8,128)S(1)} collective-permute-done((f32[2,256,256]{2,1,0:T(8,128)S(1)}, f32[2,256,256]{2,1,0:T(8,128)S(1)}, u32[]{:S(2)}, u32[]{:S(2)}) %collective-permute-start.5) | collective-permute-done | bytes 524320 | tf_op jit(solution)/shard_map/ppermute | solution.py:13
  125.4 7.9 %collective-permute-done.4 = f32[2,256,256]{2,1,0:T(8,128)S(1)} collective-permute-done((f32[2,256,256]{2,1,0:T(8,128)S(1)}, f32[2,256,256]{2,1,0:T(8,128)S(1)}, u32[]{:S(2)}, u32[]{:S(2)}) %collective-permute-start.4) | collective-permute-done | bytes 524320 | tf_op jit(solution)/shard_map/ppermute | solution.py:13
  136.6 4.1 subtract_select_fusion.3
  145.1 33.0 %collective-permute-done.8 = f32[2,256,256]{2,1,0:T(8,128)S(1)} collective-permute-done((f32[2,256,256]{2,1,0:T(8,128)S(1)}, f32[2,256,256]{2,1,0:T(8,128)S(1)}, u32[]{:S(2)}, u32[]{:S(2)}) %collective-permute-start.8) | collective-permute-done | bytes 524320 | tf_op jit(solution)/shard_map/ppermute | solution.py:13
  179.5 7.3 %collective-permute-done.7 = f32[2,256,256]{2,1,0:T(8,128)S(1)} collective-permute-done((f32[2,256,256]{2,1,0:T(8,128)S(1)}, f32[2,256,256]{2,1,0:T(8,128)S(1)}, u32[]{:S(2)}, u32[]{:S(2)}) %collective-permute-start.7) | collective-permute-done | bytes 524320 | tf_op jit(solution)/shard_map/ppermute | solution.py:13
  190.1 4.1 subtract_select_fusion.2
  194.2 3.8 collective-permute-start.9
  198.1 3.7 collective-permute-start.10
  201.8 31.6 %collective-permute-done.11 = f32[2,256,256]{2,1,0:T(8,128)} collective-permute-done((f32[2,256,256]{2,1,0:T(8,128)S(1)}, f32[2,256,256]{2,1,0:T(8,128)}, u32[]{:S(2)}, u32[]{:S(2)}) %collective-permute-start.11) | collective-permute-done | bytes 524320 | tf_op jit(solution)/shard_map/ppermute | solution.py:13
  236.1 5.1 collective-permute-done.10
  241.2 3.0 fusion.34
  245.4 4.9 broadcast_select_fusion
  251.2 87.7 %all-reduce.2.cloned.1.call-done = f32[2,128,512]{1,2,0:T(8,128)} async-done(((f32[2,128,512]{1,2,0:T(8,128)}), f32[2,128,512]{1,2,0:T(8,128)}) %all-reduce.2.cloned.1.call-update) | async-done | bytes 524304 | tf_op jit(solution)/shard_map/psum | solution.py:18
  342.7 5.1 all-to-all-start
  348.3 49.2 %all-to-all-done = f32[8,2,128,512]{3,2,1,0:T(8,128)} async-done(((f32[8,2,128,512]{3,2,1,0:T(8,128)}), f32[8,2,128,512]{3,2,1,0:T(8,128)}, u32[]{:S(2)}, u32[]{:S(2)}) %all-to-all-start) | async-done | bytes 4194336 | tf_op jit(solution)/shard_map/all_to_all | solution.py:84
  400.3 3.5 fusion.22
  410.4 17.4 %collective-permute-done.14 = f32[1,256,256]{2,1,0:T(8,128)S(1)} collective-permute-done((f32[1,256,256]{2,1,0:T(8,128)S(1)}, f32[1,256,256]{2,1,0:T(8,128)S(1)}, u32[]{:S(2)}, u32[]{:S(2)}) %collective-permute-start.14) | collective-permute-done | bytes 262176 | tf_op jit(solution)/shard_map/ppermute | solution.py:13
  441.2 16.2 %collective-permute-done.17 = f32[1,256,256]{2,1,0:T(8,128)} collective-permute-done((f32[1,256,256]{2,1,0:T(8,128)S(1)}, f32[1,256,256]{2,1,0:T(8,128)}, u32[]{:S(2)}, u32[]{:S(2)}) %collective-permute-start.17) | collective-permute-done | bytes 262176 | tf_op jit(solution)/shard_map/ppermute | solution.py:13
  467.6 16.9 %collective-permute-done.20 = f32[1,256,256]{2,1,0:T(8,128)S(1)} collective-permute-done((f32[1,256,256]{2,1,0:T(8,128)S(1)}, f32[1,256,256]{2,1,0:T(8,128)S(1)}, u32[]{:S(2)}, u32[]{:S(2)}) %collective-permute-start.20) | collective-permute-done | bytes 262176 | tf_op jit(solution)/shard_map/ppermute | solution.py:13
  498.7 4.8 pad_maximum_fusion
  503.5 5.4 %copy.92 = f32[2,1024,512]{2,1,0:T(8,128)} copy(f32[2,1024,512]{1,2,0:T(8,128)} %pad_maximum_fusion) | data formatting | bytes 8388608
  508.9 2.9 collective-permute-done.23
  (136 shorter events, 86.1 us)
Async XLA Ops:
  7.2 5.6 %copy-start = (f32[2,1024,256]{2,1,0:T(8,128)S(1)}, f32[2,1024,256]{2,1,0:T(8,128)}, u32[]{:S(2)}) copy-start(f32[2,1024,256]{2,1,0:T(8,128)} %param.15) | copy-start | bytes 6291460
  7.2 331.7 %all-reduce.2.cloned.1.call-start = ((), (), s32[]{:S(2)}) async-start(), calls=%async_computation.1 | async-start | bytes 1048576 | tf_op jit(solution)/shard_map/psum | solution.py:18
  12.7 8.6 %copy-start.23 = (f32[2,1,256,256]{3,2,1,0:T(8,128)S(1)}, f32[2,1,256,256]{3,2,1,0:T(8,128)}, u32[]{:S(2)}) copy-start(f32[2,1,256,256]{3,2,1,0:T(8,128)} %param.16) | copy-start | bytes 1572868
  29.2 37.5 %collective-permute-start = (f32[2,256,512]{1,2,0:T(8,128)}, f32[2,256,512]{1,2,0:T(8,128)S(1)}, u32[]{:S(2)}, u32[]{:S(2)}) collective-permute-start(f32[2,256,512]{1,2,0:T(8,128)} %slice.20), channel_id=1, source_target_pairs={{0,1},{1,0},{2,3},{3,2},{4,5},{5,4},{6,7},{7,6},{8,9},{9,8},{10,11... | collective-permute-start | bytes 3145736 | tf_op jit(solution)/shard_map/ppermute | solution.py:13
  30.8 35.9 %collective-permute-start.2 = (f32[2,256,256]{2,1,0:T(8,128)S(1)}, f32[2,256,256]{2,1,0:T(8,128)S(1)}, u32[]{:S(2)}, u32[]{:S(2)}) collective-permute-start(f32[2,256,256]{2,1,0:T(8,128)S(1)} %bitcast.284), channel_id=1, source_target_pairs={{0,1},{1,0},{2,3},{3,2},{4,5},{5,4},{6,7},{7,6},{8,9},{9,8},{10,11... | collective-permute-start | bytes 1572872 | tf_op jit(solution)/shard_map/ppermute | solution.py:13
  32.1 44.7 %collective-permute-start.1 = (f32[2,256,256]{2,1,0:T(8,128)S(1)}, f32[2,256,256]{2,1,0:T(8,128)}, u32[]{:S(2)}, u32[]{:S(2)}) collective-permute-start(f32[2,256,256]{2,1,0:T(8,128)S(1)} %bitcast.292), channel_id=1, source_target_pairs={{0,1},{1,0},{2,3},{3,2},{4,5},{5,4},{6,7},{7,6},{8,9},{9,8},{10,11... | collective-permute-start | bytes 1572872 | tf_op jit(solution)/shard_map/ppermute | solution.py:13
  85.2 38.9 %collective-permute-start.3 = (f32[2,256,512]{1,2,0:T(8,128)S(1)}, f32[2,256,512]{1,2,0:T(8,128)S(1)}, u32[]{:S(2)}, u32[]{:S(2)}) collective-permute-start(f32[2,256,512]{1,2,0:T(8,128)S(1)} %subtract_select_fusion.4), channel_id=1, source_target_pairs={{0,2},{1,3},{2,0},{3,1},{4,6},{5,7},{6,4},{7,5},{8,10},{9,11},{10,... | collective-permute-start | bytes 3145736 | tf_op jit(solution)/shard_map/ppermute | solution.py:13
  88.5 35.5 %collective-permute-start.5 = (f32[2,256,256]{2,1,0:T(8,128)S(1)}, f32[2,256,256]{2,1,0:T(8,128)S(1)}, u32[]{:S(2)}, u32[]{:S(2)}) collective-permute-start(f32[2,256,256]{2,1,0:T(8,128)S(1)} %bitcast.285), channel_id=1, source_target_pairs={{0,2},{1,3},{2,0},{3,1},{4,6},{5,7},{6,4},{7,5},{8,10},{9,11},{10,... | collective-permute-start | bytes 1572872 | tf_op jit(solution)/shard_map/ppermute | solution.py:13
  88.8 44.5 %collective-permute-start.4 = (f32[2,256,256]{2,1,0:T(8,128)S(1)}, f32[2,256,256]{2,1,0:T(8,128)S(1)}, u32[]{:S(2)}, u32[]{:S(2)}) collective-permute-start(f32[2,256,256]{2,1,0:T(8,128)S(1)} %bitcast.293), channel_id=1, source_target_pairs={{0,2},{1,3},{2,0},{3,1},{4,6},{5,7},{6,4},{7,5},{8,10},{9,11},{10,... | collective-permute-start | bytes 1572872 | tf_op jit(solution)/shard_map/ppermute | solution.py:13
  140.7 37.5 %collective-permute-start.6 = (f32[2,256,512]{1,2,0:T(8,128)S(1)}, f32[2,256,512]{1,2,0:T(8,128)S(1)}, u32[]{:S(2)}, u32[]{:S(2)}) collective-permute-start(f32[2,256,512]{1,2,0:T(8,128)S(1)} %subtract_select_fusion.3), channel_id=1, source_target_pairs={{0,4},{1,5},{2,6},{3,7},{4,0},{5,1},{6,2},{7,3},{8,12},{9,13},{10,... | collective-permute-start | bytes 3145736 | tf_op jit(solution)/shard_map/ppermute | solution.py:13
  142.9 35.2 %collective-permute-start.8 = (f32[2,256,256]{2,1,0:T(8,128)S(1)}, f32[2,256,256]{2,1,0:T(8,128)S(1)}, u32[]{:S(2)}, u32[]{:S(2)}) collective-permute-start(f32[2,256,256]{2,1,0:T(8,128)S(1)} %bitcast.286), channel_id=1, source_target_pairs={{0,4},{1,5},{2,6},{3,7},{4,0},{5,1},{6,2},{7,3},{8,12},{9,13},{10,... | collective-permute-start | bytes 1572872 | tf_op jit(solution)/shard_map/ppermute | solution.py:13
  143.2 43.6 %collective-permute-start.7 = (f32[2,256,256]{2,1,0:T(8,128)S(1)}, f32[2,256,256]{2,1,0:T(8,128)S(1)}, u32[]{:S(2)}, u32[]{:S(2)}) collective-permute-start(f32[2,256,256]{2,1,0:T(8,128)S(1)} %bitcast.294), channel_id=1, source_target_pairs={{0,4},{1,5},{2,6},{3,7},{4,0},{5,1},{6,2},{7,3},{8,12},{9,13},{10,... | collective-permute-start | bytes 1572872 | tf_op jit(solution)/shard_map/ppermute | solution.py:13
  194.2 39.1 %collective-permute-start.9 = (f32[2,256,512]{1,2,0:T(8,128)S(1)}, f32[2,256,512]{1,2,0:T(8,128)S(1)}, u32[]{:S(2)}, u32[]{:S(2)}) collective-permute-start(f32[2,256,512]{1,2,0:T(8,128)S(1)} %subtract_select_fusion.2), channel_id=1, source_target_pairs={{0,8},{1,9},{2,10},{3,11},{4,12},{5,13},{6,14},{7,15},{8,0},{9,1},... | collective-permute-start | bytes 3145736 | tf_op jit(solution)/shard_map/ppermute | solution.py:13
  198.0 35.3 %collective-permute-start.11 = (f32[2,256,256]{2,1,0:T(8,128)S(1)}, f32[2,256,256]{2,1,0:T(8,128)}, u32[]{:S(2)}, u32[]{:S(2)}) collective-permute-start(f32[2,256,256]{2,1,0:T(8,128)S(1)} %bitcast.287), channel_id=1, source_target_pairs={{0,8},{1,9},{2,10},{3,11},{4,12},{5,13},{6,14},{7,15},{8,0},{9,1},... | collective-permute-start | bytes 1572872 | tf_op jit(solution)/shard_map/ppermute | solution.py:13
  198.1 43.1 %collective-permute-start.10 = (f32[2,256,256]{2,1,0:T(8,128)S(1)}, f32[2,256,256]{2,1,0:T(8,128)}, u32[]{:S(2)}, u32[]{:S(2)}) collective-permute-start(f32[2,256,256]{2,1,0:T(8,128)S(1)} %bitcast.295), channel_id=1, source_target_pairs={{0,8},{1,9},{2,10},{3,11},{4,12},{5,13},{6,14},{7,15},{8,0},{9,1},... | collective-permute-start | bytes 1572872 | tf_op jit(solution)/shard_map/ppermute | solution.py:13
  342.7 5.2 copy-start.28
  342.7 5.3 %copy-start.25 = (s32[16,128]{1,0:T(8,128)S(1)}, s32[16,128]{1,0:T(8,128)}, u32[]{:S(2)}) copy-start(s32[16,128]{1,0:T(8,128)} %param.22) | copy-start | bytes 24580
  342.7 54.8 %all-to-all-start = ((f32[8,2,128,512]{3,2,1,0:T(8,128)}), f32[8,2,128,512]{3,2,1,0:T(8,128)}, u32[]{:S(2)}, u32[]{:S(2)}) async-start(f32[8,2,128,512]{3,2,1,0:T(8,128)} %stack.2), calls=%async_computation | async-start | bytes 8388608 | tf_op jit(solution)/shard_map/all_to_all | solution.py:84
  407.2 20.6 %collective-permute-start.12 = (f32[1,256,512]{2,1,0:T(8,128)}, f32[1,256,512]{2,1,0:T(8,128)S(1)}, u32[]{:S(2)}, u32[]{:S(2)}) collective-permute-start(f32[1,256,512]{2,1,0:T(8,128)} %slice.23), channel_id=1, source_target_pairs={{0,1},{1,0},{2,3},{3,2},{4,5},{5,4},{6,7},{7,6},{8,9},{9,8},{10,11... | collective-permute-start | bytes 1572872 | tf_op jit(solution)/shard_map/ppermute | solution.py:13
  408.4 25.2 %copy-start.7 = (f32[1,1024,512]{2,1,0:T(8,128)S(1)}, f32[1,1024,512]{2,1,0:T(8,128)}, u32[]{:S(2)}) copy-start(f32[1,1024,512]{2,1,0:T(8,128)} %copy-done.6) | copy-start | bytes 6291460
  408.4 19.4 %collective-permute-start.14 = (f32[1,256,256]{2,1,0:T(8,128)S(1)}, f32[1,256,256]{2,1,0:T(8,128)S(1)}, u32[]{:S(2)}, u32[]{:S(2)}) collective-permute-start(f32[1,256,256]{2,1,0:T(8,128)S(1)} %bitcast.288), channel_id=1, source_target_pairs={{0,1},{1,0},{2,3},{3,2},{4,5},{5,4},{6,7},{7,6},{8,9},{9,8},{10,11... | collective-permute-start | bytes 786440 | tf_op jit(solution)/shard_map/ppermute | solution.py:13
  409.2 22.8 %collective-permute-start.13 = (f32[1,256,256]{2,1,0:T(8,128)}, f32[1,256,256]{2,1,0:T(8,128)S(1)}, u32[]{:S(2)}, u32[]{:S(2)}) collective-permute-start(f32[1,256,256]{2,1,0:T(8,128)} %bitcast.12), channel_id=1, source_target_pairs={{0,1},{1,0},{2,3},{3,2},{4,5},{5,4},{6,7},{7,6},{8,9},{9,8},{10,11... | collective-permute-start | bytes 786440 | tf_op jit(solution)/shard_map/ppermute | solution.py:13
  435.3 22.1 %collective-permute-start.15 = (f32[1,256,512]{2,1,0:T(8,128)S(1)}, f32[1,256,512]{2,1,0:T(8,128)S(1)}, u32[]{:S(2)}, u32[]{:S(2)}) collective-permute-start(f32[1,256,512]{2,1,0:T(8,128)S(1)} %fusion.30), channel_id=1, source_target_pairs={{0,2},{1,3},{2,0},{3,1},{4,6},{5,7},{6,4},{7,5},{8,10},{9,11},{10,... | collective-permute-start | bytes 1572872 | tf_op jit(solution)/shard_map/ppermute | solution.py:13
  437.5 19.9 %collective-permute-start.17 = (f32[1,256,256]{2,1,0:T(8,128)S(1)}, f32[1,256,256]{2,1,0:T(8,128)}, u32[]{:S(2)}, u32[]{:S(2)}) collective-permute-start(f32[1,256,256]{2,1,0:T(8,128)S(1)} %bitcast.289), channel_id=1, source_target_pairs={{0,2},{1,3},{2,0},{3,1},{4,6},{5,7},{6,4},{7,5},{8,10},{9,11},{10,... | collective-permute-start | bytes 786440 | tf_op jit(solution)/shard_map/ppermute | solution.py:13
  439.0 21.8 %collective-permute-start.16 = (f32[1,256,256]{2,1,0:T(8,128)}, f32[1,256,256]{2,1,0:T(8,128)}, u32[]{:S(2)}, u32[]{:S(2)}) collective-permute-start(f32[1,256,256]{2,1,0:T(8,128)} %bitcast.12), channel_id=1, source_target_pairs={{0,2},{1,3},{2,0},{3,1},{4,6},{5,7},{6,4},{7,5},{8,10},{9,11},{10,... | collective-permute-start | bytes 786440 | tf_op jit(solution)/shard_map/ppermute | solution.py:13
  464.4 20.9 %collective-permute-start.18 = (f32[1,256,512]{2,1,0:T(8,128)S(1)}, f32[1,256,512]{2,1,0:T(8,128)}, u32[]{:S(2)}, u32[]{:S(2)}) collective-permute-start(f32[1,256,512]{2,1,0:T(8,128)S(1)} %fusion.28), channel_id=1, source_target_pairs={{0,4},{1,5},{2,6},{3,7},{4,0},{5,1},{6,2},{7,3},{8,12},{9,13},{10,... | collective-permute-start | bytes 1572872 | tf_op jit(solution)/shard_map/ppermute | solution.py:13
  465.6 18.9 %collective-permute-start.20 = (f32[1,256,256]{2,1,0:T(8,128)S(1)}, f32[1,256,256]{2,1,0:T(8,128)S(1)}, u32[]{:S(2)}, u32[]{:S(2)}) collective-permute-start(f32[1,256,256]{2,1,0:T(8,128)S(1)} %bitcast.290), channel_id=1, source_target_pairs={{0,4},{1,5},{2,6},{3,7},{4,0},{5,1},{6,2},{7,3},{8,12},{9,13},{10,... | collective-permute-start | bytes 786440 | tf_op jit(solution)/shard_map/ppermute | solution.py:13
  466.5 21.0 %collective-permute-start.19 = (f32[1,256,256]{2,1,0:T(8,128)}, f32[1,256,256]{2,1,0:T(8,128)}, u32[]{:S(2)}, u32[]{:S(2)}) collective-permute-start(f32[1,256,256]{2,1,0:T(8,128)} %bitcast.12), channel_id=1, source_target_pairs={{0,4},{1,5},{2,6},{3,7},{4,0},{5,1},{6,2},{7,3},{8,12},{9,13},{10,... | collective-permute-start | bytes 786440 | tf_op jit(solution)/shard_map/ppermute | solution.py:13
  487.2 9.5 %copy-start.4 = (f32[2,1024,512]{1,2,0:T(8,128)S(1)}, f32[2,1024,512]{1,2,0:T(8,128)}, u32[]{:S(2)}) copy-start(f32[2,1024,512]{1,2,0:T(8,128)} %copy-done.3) | copy-start | bytes 12582916
  491.1 20.7 %collective-permute-start.21 = (f32[1,256,512]{2,1,0:T(8,128)S(1)}, f32[1,256,512]{2,1,0:T(8,128)S(1)}, u32[]{:S(2)}, u32[]{:S(2)}) collective-permute-start(f32[1,256,512]{2,1,0:T(8,128)S(1)} %fusion.26), channel_id=1, source_target_pairs={{0,8},{1,9},{2,10},{3,11},{4,12},{5,13},{6,14},{7,15},{8,0},{9,1},... | collective-permute-start | bytes 1572872 | tf_op jit(solution)/shard_map/ppermute | solution.py:13
  493.2 18.5 %collective-permute-start.23 = (f32[1,256,256]{2,1,0:T(8,128)S(1)}, f32[1,256,256]{2,1,0:T(8,128)}, u32[]{:S(2)}, u32[]{:S(2)}) collective-permute-start(f32[1,256,256]{2,1,0:T(8,128)S(1)} %bitcast.291), channel_id=1, source_target_pairs={{0,8},{1,9},{2,10},{3,11},{4,12},{5,13},{6,14},{7,15},{8,0},{9,1},... | collective-permute-start | bytes 786440 | tf_op jit(solution)/shard_map/ppermute | solution.py:13
  494.7 19.9 %collective-permute-start.22 = (f32[1,256,256]{2,1,0:T(8,128)}, f32[1,256,256]{2,1,0:T(8,128)}, u32[]{:S(2)}, u32[]{:S(2)}) collective-permute-start(f32[1,256,256]{2,1,0:T(8,128)} %bitcast.12), channel_id=1, source_target_pairs={{0,8},{1,9},{2,10},{3,11},{4,12},{5,13},{6,14},{7,15},{8,0},{9,1},... | collective-permute-start | bytes 786440 | tf_op jit(solution)/shard_map/ppermute | solution.py:13
  (24 other events, 63.2 us)
Sparse Core Ops, SparseCore 0:
  251.3 87.5 all-reduce.1
